TPU v7x, 256 devices: a whole 4x4x8 slice. The times are simulated.
256 devices in a mesh: tiles: 64 (over y, x_lo, z), probes: 4 (over x_hi, core).
Axes of the slice: x: 4 (x_hi: 2, x_lo: 2; x = x_hi * 2 + x_lo), y: 4, z: 8, core: 2. Of those that a mesh axis runs over, the one named last changes fastest.
Arguments:
- blocks: bfloat16 [4096, 192, 192], P('tiles'), may hold values from -0.21875 to 0.21875
- connectivity: int32 [4096, 64], P('tiles'), may hold values from 0 to 4607, as said below
- basal_map: int32 [4096, 64], P('tiles'), may hold values from 0 to 383
- friction: float32 [4096, 64, 3], P('tiles'), may hold values from 0.2 to 2
- elem_counts: int32 [64], P('tiles'), may hold values from 1 to 64, 3072 in all
- obs_weight: float32 [262144, 3], P('tiles'), may hold values from 0.2 to 2
- sign_bits: int32 [16384, 32], P('tiles', 'probes'), may hold values from 0 to 1
- cluster_ids: int32 [16384], P('tiles'), may hold values from 0 to 63, never falling along the last dimension, each value on 1 to 512 neighbouring positions
Outputs:
- samples: float32 [16384, 32], P('tiles', 'probes')
- refined: float32 [16384, 32], P('tiles', 'probes')
- gram: float32 [64, 32, 32], P(None, 'probes')
Inputs may be any that keep to these rules, and one draw needn't show every extreme that they name: `connectivity`: about one reference in eight names a node of the next tile. `elem_counts`: some tile has all 64 slots live. `cluster_ids`: never falling along the cells; each cluster holds 1 to 512 cells.
All inputs are finite; a program needn't handle non-finite values. No bound on the sum of `elem_counts` on one device may be relied on, other than what follows from the above.
Results may differ from a plain program's by a relative error of at most 0.004.
Values may be sent and summed in bfloat16 or wider, within the bound.
A program may use at most 64 MiB of HBM per device.

v0:
```python
import jax
import jax.numpy as jnp
from jax import lax
from jax.sharding import PartitionSpec as P

HALO = 512
POWER = 2
RIM = 64


def padded(x, sides, width):
    for axis, dim in sides:
        size, length = (lax.axis_size(axis), x.shape[dim])
        up = [(i, (i + 1) % size) for i in range(size - 1)]
        down = [(j, i) for i, j in up]
        last = lax.slice_in_dim(x, length - width, length, axis=dim)
        leading = lax.slice_in_dim(x, 0, width, axis=dim)
        before = lax.ppermute(last, axis, up)
        after = lax.ppermute(leading, axis, down)
        x = jnp.concatenate([before, x, after], axis=dim)
    return x


def from_behind(block, axis, distance):
    devices = range(lax.axis_size(axis))
    route = [(i - distance, i) for i in devices if i - distance in devices]
    return lax.ppermute(block, axis, route)


def shards(
    blocks, connectivity, basal_map, friction, elem_counts, obs_weight, sign_bits, cluster_ids
):
    elem_slots = blocks.shape[0]
    block_order = blocks.shape[1]
    node_slots = connectivity.shape[1]
    node_count = obs_weight.shape[0]
    halo_nodes = HALO
    rim_cells = RIM
    cell_count = sign_bits.shape[0]
    group_size = sign_bits.shape[1]
    tile_count = lax.axis_size("tiles")
    alive_slots = jnp.arange(elem_slots, dtype=jnp.int32) < elem_counts[0]
    flat_nodes = connectivity.reshape(-1)
    flat_cells = basal_map.reshape(-1)

    def hessian(probe_field):
        window = padded(probe_field, (("tiles", 0),), rim_cells)
        picked = window[basal_map]
        inputs = (friction[:, :, :, None] * picked[:, :, None, :]).astype(jnp.bfloat16)
        inputs = inputs.reshape(elem_slots, block_order, group_size)
        forward = jnp.einsum("eij,ejp->eip", blocks, inputs, preferred_element_type=jnp.float32)
        forward = jnp.where(alive_slots[:, None, None], forward, jnp.float32(0.0))
        summed = jax.ops.segment_sum(
            forward.reshape(elem_slots * node_slots, 3 * group_size),
            flat_nodes,
            num_segments=node_count + halo_nodes,
        )
        owned_sum = summed[:node_count]
        spilled = summed[node_count:]
        returned = from_behind(spilled, "tiles", 1)
        owned_sum = jnp.concatenate([owned_sum[:halo_nodes] + returned, owned_sum[halo_nodes:]], 0)
        weighted = (obs_weight[:, :, None] * owned_sum.reshape(node_count, 3, group_size)).astype(
            jnp.bfloat16
        )
        weighted = weighted.reshape(node_count, 3 * group_size)
        weighted_rim = from_behind(weighted[:halo_nodes], "tiles", -1)
        node_window = jnp.concatenate([weighted, weighted_rim], 0)
        adjoint_in = node_window[connectivity].reshape(elem_slots, block_order, group_size)
        adjoint_out = jnp.einsum(
            "eji,ejp->eip", blocks, adjoint_in, preferred_element_type=jnp.float32
        )
        partials = jnp.sum(
            friction[:, :, :, None] * adjoint_out.reshape(elem_slots, node_slots, 3, group_size),
            axis=2,
        )
        partials = jnp.where(alive_slots[:, None, None], partials, jnp.float32(0.0))
        basal = jax.ops.segment_sum(
            partials.reshape(elem_slots * node_slots, group_size),
            flat_cells,
            num_segments=cell_count + 2 * rim_cells,
        )
        from_next = from_behind(basal[:rim_cells], "tiles", -1)
        from_prev = from_behind(basal[cell_count + rim_cells :], "tiles", 1)
        middle = basal[rim_cells : cell_count + rim_cells]
        middle = middle + jnp.pad(from_prev, ((0, cell_count - rim_cells), (0, 0)))
        middle = middle + jnp.pad(from_next, ((cell_count - rim_cells, 0), (0, 0)))
        return middle

    parity = jnp.arange(group_size, dtype=jnp.int32) % 2
    same_colour = (cluster_ids % 2)[:, None] == parity[None, :]
    probe_start = jnp.where(same_colour, (2 * sign_bits - 1).astype(jnp.float32), jnp.float32(0.0))
    samples = jnp.where(same_colour, jnp.float32(0.0), hessian(probe_start))
    current = samples
    for power_step in range(POWER):
        squares = lax.psum(jnp.sum(current * current, axis=0), "tiles")
        rms_scale = jnp.sqrt(squares / (cell_count * tile_count) + 1e-06)
        applied = hessian(current / rms_scale)
        if power_step % 2 == 0:
            current = jnp.where(same_colour, applied, jnp.float32(0.0))
        else:
            current = jnp.where(same_colour, jnp.float32(0.0), applied)
    onehot = (cluster_ids[:, None] == jnp.arange(tile_count, dtype=jnp.int32)[None, :]).astype(
        jnp.float32
    )
    column_block = lax.all_gather(current, "probes", axis=1, tiled=True)
    outer = current[:, :, None] * column_block[:, None, :]
    width = column_block.shape[1]
    result = jnp.dot(
        onehot.T, outer.reshape(cell_count, group_size * width), precision=lax.Precision.HIGHEST
    )
    partial_gram = result.reshape(tile_count, group_size, width)
    gram = lax.psum(partial_gram, "tiles")
    return (samples, current, gram)


def solution(mesh):
    in_specs = (
        P("tiles", None, None),
        P("tiles", None),
        P("tiles", None),
        P("tiles", None, None),
        P("tiles"),
        P("tiles", None),
        P("tiles", "probes"),
        P("tiles"),
    )
    out_specs = (P("tiles", "probes"), P("tiles", "probes"), P(None, "probes", None))
    return jax.shard_map(shards, mesh=mesh, in_specs=in_specs, out_specs=out_specs, check_vma=False)
```

profile of v0, /device:TPU:4, one launch (start us, length us, event | category | flops | bytes accessed | tf_op | source)
XLA Modules:
  0.0 1263.8 jit_solution(13736577192659652602)
XLA Ops:
  18.3 10.8 gather_fusion
  39.1 5.3 reshape.163
  44.4 23.2 %scatter_custom_fusion = f32[4608,24]{1,0:T(8,128)S(1)} fusion(s32[4096]{0:T(1024)S(1)} %reshape.161, f32[4096,24]{1,0:T(8,128)} %reshape.163, f32[]{:T(128)} %constant.39.clone.1), kind=kCustom, calls=%fused_computation.25 | custom fusion | flops 98304 | bytes 442880 | tf_op jit(solution)/shard_map/scatter-add | solution.py:53
  79.3 4.7 collective-permute-done.3
  84.6 14.9 %gather_fusion.1 = bf16[4096,24]{1,0:T(8,128)(2,1)} fusion(bf16[4608,24]{1,0:T(8,128)(2,1)S(1)} %copy.180, s32[4096]{0:T(1024)S(1)} %broadcast_clamp_fusion), kind=kCustom, calls=%fused_computation.1 | custom fusion | bytes 409600 | tf_op jit(solution)/shard_map/gather | solution.py:68
  103.2 4.6 convolution_bitcast_fusion.2
  110.2 22.4 %scatter_custom_fusion.1 = f32[384,8]{1,0:T(8,128)S(1)} fusion(s32[4096]{0:T(1024)S(1)} %reshape.169, f32[4096,8]{1,0:T(8,128)S(1)} %copy.184, f32[]{:T(128)} %constant.39.clone.1), kind=kCustom, calls=%fused_computation.63 | custom fusion | flops 32768 | bytes 12292 | tf_op jit(solution)/shard_map/scatter-add | solution.py:77
  134.0 5.2 collective-permute-start.4
  140.8 161.9 %psum.21 = f32[8]{0:T(128)S(1)} all-reduce(f32[8]{0:T(128)S(1)} %get-tuple-element.15), channel_id=1, replica_groups=mesh['tiles'=64,'probes'=4] {'tiles'}, use_global_device_ids=true, to_apply=%region_4.5 | all-reduce | flops 8 | bytes 64 | tf_op jit(solution)/shard_map/psum | solution.py:95
  309.8 10.8 gather_fusion.2
  330.7 5.3 reshape.179
  335.9 23.2 %scatter_custom_fusion.2 = f32[4608,24]{1,0:T(8,128)S(1)} fusion(s32[4096]{0:T(1024)S(1)} %reshape.161, f32[4096,24]{1,0:T(8,128)} %reshape.179, f32[]{:T(128)} %constant.39.clone.1), kind=kCustom, calls=%fused_computation.23 | custom fusion | flops 98304 | bytes 442880 | tf_op jit(solution)/shard_map/scatter-add | solution.py:53
  367.4 4.8 collective-permute-done.9
  372.7 14.9 %gather_fusion.3 = bf16[4096,24]{1,0:T(8,128)(2,1)} fusion(bf16[4608,24]{1,0:T(8,128)(2,1)S(1)} %copy.194, s32[4096]{0:T(1024)S(1)} %broadcast_clamp_fusion), kind=kCustom, calls=%fused_computation.3 | custom fusion | bytes 409600 | tf_op jit(solution)/shard_map/gather | solution.py:68
  398.3 22.4 %scatter_custom_fusion.3 = f32[384,8]{1,0:T(8,128)S(1)} fusion(s32[4096]{0:T(1024)S(1)} %reshape.169, f32[4096,8]{1,0:T(8,128)S(1)} %copy.198, f32[]{:T(128)} %constant.39.clone.1), kind=kCustom, calls=%fused_computation.61 | custom fusion | flops 32768 | bytes 12292 | tf_op jit(solution)/shard_map/scatter-add | solution.py:77
  428.2 157.2 %psum.22 = f32[8]{0:T(128)S(1)} all-reduce(f32[8]{0:T(128)S(1)} %multiply_reduce_fusion.3), channel_id=1, replica_groups=mesh['tiles'=64,'probes'=4] {'tiles'}, use_global_device_ids=true, to_apply=%region_9.10 | all-reduce | flops 8 | bytes 64 | tf_op jit(solution)/shard_map/psum | solution.py:95
  592.6 10.8 gather_fusion.4
  613.5 5.3 reshape.195
  618.7 23.2 %scatter_custom_fusion.4 = f32[4608,24]{1,0:T(8,128)S(1)} fusion(s32[4096]{0:T(1024)S(1)} %reshape.161, f32[4096,24]{1,0:T(8,128)} %reshape.195, f32[]{:T(128)} %constant.39.clone.1), kind=kCustom, calls=%fused_computation.21 | custom fusion | flops 98304 | bytes 442880 | tf_op jit(solution)/shard_map/scatter-add | solution.py:53
  650.2 4.8 collective-permute-done.15
  655.5 14.9 %gather_fusion.5 = bf16[4096,24]{1,0:T(8,128)(2,1)} fusion(bf16[4608,24]{1,0:T(8,128)(2,1)S(1)} %copy.208, s32[4096]{0:T(1024)S(1)} %broadcast_clamp_fusion), kind=kCustom, calls=%fused_computation.5 | custom fusion | bytes 409600 | tf_op jit(solution)/shard_map/gather | solution.py:68
  681.1 22.4 %scatter_custom_fusion.5 = f32[384,8]{1,0:T(8,128)S(1)} fusion(s32[4096]{0:T(1024)S(1)} %reshape.169, f32[4096,8]{1,0:T(8,128)S(1)} %copy.212, f32[]{:T(128)} %constant.39.clone.1), kind=kCustom, calls=%fused_computation.59 | custom fusion | flops 32768 | bytes 12292 | tf_op jit(solution)/shard_map/scatter-add | solution.py:77
  710.9 6.7 all_gather.3
  718.5 536.8 %all-reduce.8.cloned.1.call-done = f32[64,8,32]{0,2,1:T(8,128)} async-done(((f32[64,8,32]{0,2,1:T(8,128)}), f32[64,8,32]{0,2,1:T(8,128)}) %all-reduce.8.cloned.1.call-update) | async-done | bytes 65552 | tf_op jit(solution)/shard_map/psum | solution.py:112
  (161 shorter events, 132.0 us)
Async XLA Ops:
  7.2 1248.2 %all-reduce.8.cloned.1.call-start = ((), (), s32[]{:S(2)}) async-start(), calls=%async_computation | async-start | bytes 262144 | tf_op jit(solution)/shard_map/psum | solution.py:112
  8.8 8.5 collective-permute-start
  12.6 5.5 collective-permute-start.1
  44.4 27.8 %copy-start.1 = (s32[64,64]{1,0:T(8,128)S(1)}, s32[64,64]{1,0:T(8,128)}, u32[]{:S(2)}) copy-start(s32[64,64]{1,0:T(8,128)} %param.9) | copy-start | bytes 49156
  44.4 27.8 %copy-start = (f32[4096,3]{0,1:T(4,128)S(1)}, f32[4096,3]{0,1:T(4,128)}, u32[]{:S(2)}) copy-start(f32[4096,3]{0,1:T(4,128)} %param.13) | copy-start | bytes 147460
  67.6 8.9 collective-permute-start.2
  77.7 6.3 collective-permute-start.3
  132.7 6.6 collective-permute-start.5
  134.0 6.5 collective-permute-start.4
  140.7 179.9 %copy-start.4 = (f32[256,8]{0,1:T(8,128)}, f32[256,8]{0,1:T(8,128)S(1)}, u32[]{:S(2)}) copy-start(f32[256,8]{0,1:T(8,128)S(1)} %get-tuple-element.35) | copy-start | bytes 24580
  302.8 2.8 collective-permute-start.6
  304.1 5.5 collective-permute-start.7
  359.2 5.7 collective-permute-start.8
  366.1 6.1 collective-permute-start.9
  420.9 5.9 collective-permute-start.11
  422.2 5.9 collective-permute-start.10
  585.6 2.8 collective-permute-start.12
  586.9 5.5 collective-permute-start.13
  642.0 5.7 collective-permute-start.14
  648.9 6.1 collective-permute-start.15
  680.2 37.4 %copy-start.5 = (s32[256]{0:T(256)S(1)}, s32[256]{0:T(256)}, u32[]{:S(2)}) copy-start(s32[256]{0:T(256)} %param.15) | copy-start | bytes 3076
  703.7 5.9 collective-permute-start.17
  705.0 5.9 collective-permute-start.16
  710.9 546.0 %copy-start.3 = (f32[256,8]{0,1:T(8,128)}, f32[256,8]{0,1:T(8,128)S(1)}, u32[]{:S(2)}) copy-start(f32[256,8]{0,1:T(8,128)S(1)} %compare_select_fusion.2) | copy-start | bytes 24580
  (1 other events, 5.4 us)
Sparse Core Ops, SparseCore 0:
  718.7 536.6 all-reduce.7
where the time goes:
time: 1270 us; the launch traced here: 1260 us
  waiting for transfers between devices  564 us (44%)
  blocking collectives  326 us (26%)
  other arithmetic  144 us (11%)
  local copies, waits for them, and re-layouts  144 us (11%)
  starting transfers between devices  42.1 us (3%)
  matrix products  28.1 us (2%)
  between operations  15.4 us (1%)
    psum x1, waiting for transfers between devices, shards(): gram = lax.psum(partial_gram, 'tiles')  537 us
    psum x2, blocking collectives, shards(): squares = lax.psum(jnp.sum(current * current, axis=0), 'tiles')  319 us
    scatter-add x3, other arithmetic, hessian(): jax.ops.segment_sum(forward.reshape(elem_slots * node_slots, 3 * group_si...  69.7 us
    scatter-add x3, other arithmetic, hessian(): jax.ops.segment_sum(partials.reshape(elem_slots * node_slots, group_size)...  67.2 us
    gather x3, local copies, waits for them, and re-layouts, hessian(): node_window[connectivity].reshape(elem_slots, block_order, group_size)  44.7 us
    gather x6, local copies, waits for them, and re-layouts, hessian(): picked = window[basal_map]  35.6 us
    ppermute x12, starting transfers between devices, from_behind(): return lax.ppermute(block, axis, route)  31.4 us
  transfers between devices with their start and end apart: 19, of which 11 were waited for; matrix products, arithmetic and copies ran while one was open for 1% of the time, Pallas kernels for 0%

commit v1 on v0

--- a/solution.py
+++ b/solution.py
@@ -92,7 +92,7 @@
     samples = jnp.where(same_colour, jnp.float32(0.0), hessian(probe_start))
     current = samples
     for power_step in range(POWER):
-        squares = lax.psum(jnp.sum(current * current, axis=0), "tiles")
+        squares = jnp.sum(lax.all_gather(jnp.sum(current * current, axis=0), "tiles"), axis=0)
         rms_scale = jnp.sqrt(squares / (cell_count * tile_count) + 1e-06)
         applied = hessian(current / rms_scale)
         if power_step % 2 == 0:

time: 1270 us -> 1260 us (level)
    psum x2 -> x0, blocking collectives: 319 us -> none  [shards(): squares = lax.psum(jnp.sum(current * current, axis=0), 'tiles')]
    unnamed x0 -> x2, blocking collectives: none -> 309 us
where the time goes in v1:
time: 1260 us
  waiting for transfers between devices  570 us (45%)
  blocking collectives  316 us (25%)
  local copies, waits for them, and re-layouts  145 us (12%)
  other arithmetic  144 us (11%)
  starting transfers between devices  42.6 us (3%)
  matrix products  28.1 us (2%)
  between operations  16.1 us (1%)
    psum x1, waiting for transfers between devices, shards(): gram = lax.psum(partial_gram, 'tiles')  534 us
    unnamed x2, blocking collectives  309 us
    scatter-add x3, other arithmetic, hessian(): jax.ops.segment_sum(forward.reshape(elem_slots * node_slots, 3 * group_si...  69.7 us
    scatter-add x3, other arithmetic, hessian(): jax.ops.segment_sum(partials.reshape(elem_slots * node_slots, group_size)...  67.2 us
    gather x3, local copies, waits for them, and re-layouts, hessian(): node_window[connectivity].reshape(elem_slots, block_order, group_size)  44.7 us
    gather x6, local copies, waits for them, and re-layouts, hessian(): picked = window[basal_map]  35.6 us
    ppermute x12, starting transfers between devices, from_behind(): return lax.ppermute(block, axis, route)  29.7 us
    ppermute x12, waiting for transfers between devices, from_behind(): return lax.ppermute(block, axis, route)  27 us
  transfers between devices with their start and end apart: 19, of which 11 were waited for; matrix products, arithmetic and copies ran while one was open for 1% of the time, Pallas kernels for 0%

profile of v1, /device:TPU:4, one launch (start us, length us, event | category | flops | bytes accessed | tf_op | source)
XLA Modules:
  0.0 1261.8 jit_solution(2645886326257581653)
XLA Ops:
  18.3 10.8 gather_fusion
  39.1 5.3 reshape.171
  44.4 23.2 %scatter_custom_fusion = f32[4608,24]{1,0:T(8,128)S(1)} fusion(s32[4096]{0:T(1024)S(1)} %reshape.169, f32[4096,24]{1,0:T(8,128)} %reshape.171, f32[]{:T(128)} %constant.39.clone.1), kind=kCustom, calls=%fused_computation.25 | custom fusion | flops 98304 | bytes 442880 | tf_op jit(solution)/shard_map/scatter-add | solution.py:53
  79.3 4.7 collective-permute-done.3
  84.6 14.9 %gather_fusion.1 = bf16[4096,24]{1,0:T(8,128)(2,1)} fusion(bf16[4608,24]{1,0:T(8,128)(2,1)S(1)} %copy.180, s32[4096]{0:T(1024)S(1)} %broadcast_clamp_fusion), kind=kCustom, calls=%fused_computation.1 | custom fusion | bytes 409600 | tf_op jit(solution)/shard_map/gather | solution.py:68
  103.2 4.6 convolution_bitcast_fusion.2
  110.2 22.4 %scatter_custom_fusion.1 = f32[384,8]{1,0:T(8,128)S(1)} fusion(s32[4096]{0:T(1024)S(1)} %reshape.177, f32[4096,8]{1,0:T(8,128)S(1)} %copy.184, f32[]{:T(128)} %constant.39.clone.1), kind=kCustom, calls=%fused_computation.63 | custom fusion | flops 32768 | bytes 12292 | tf_op jit(solution)/shard_map/scatter-add | solution.py:77
  132.7 4.6 collective-permute-start.4
  144.0 156.7 %all-reduce.6 = f32[512]{0:T(512)S(1)} all-reduce(f32[512]{0:T(512)S(1)} %dynamic-update-slice), channel_id=2, replica_groups=mesh['tiles'=64,'probes'=4] {'tiles'}, use_global_device_ids=true, to_apply=%add.6 | all-reduce | flops 512 | bytes 4096
  308.0 10.8 gather_fusion.2
  328.9 5.3 reshape.187
  334.1 23.2 %scatter_custom_fusion.2 = f32[4608,24]{1,0:T(8,128)S(1)} fusion(s32[4096]{0:T(1024)S(1)} %reshape.169, f32[4096,24]{1,0:T(8,128)} %reshape.187, f32[]{:T(128)} %constant.39.clone.1), kind=kCustom, calls=%fused_computation.23 | custom fusion | flops 98304 | bytes 442880 | tf_op jit(solution)/shard_map/scatter-add | solution.py:53
  365.6 4.8 collective-permute-done.9
  370.9 14.9 %gather_fusion.3 = bf16[4096,24]{1,0:T(8,128)(2,1)} fusion(bf16[4608,24]{1,0:T(8,128)(2,1)S(1)} %copy.194, s32[4096]{0:T(1024)S(1)} %broadcast_clamp_fusion), kind=kCustom, calls=%fused_computation.3 | custom fusion | bytes 409600 | tf_op jit(solution)/shard_map/gather | solution.py:68
  396.5 22.4 %scatter_custom_fusion.3 = f32[384,8]{1,0:T(8,128)S(1)} fusion(s32[4096]{0:T(1024)S(1)} %reshape.177, f32[4096,8]{1,0:T(8,128)S(1)} %copy.198, f32[]{:T(128)} %constant.39.clone.1), kind=kCustom, calls=%fused_computation.61 | custom fusion | flops 32768 | bytes 12292 | tf_op jit(solution)/shard_map/scatter-add | solution.py:77
  428.9 152.7 %all-reduce.7 = f32[512]{0:T(512)S(1)} all-reduce(f32[512]{0:T(512)S(1)} %dynamic-update-slice.1), channel_id=3, replica_groups=mesh['tiles'=64,'probes'=4] {'tiles'}, use_global_device_ids=true, to_apply=%add.7 | all-reduce | flops 512 | bytes 4096
  591.2 10.8 gather_fusion.4
  612.1 5.3 reshape.203
  617.3 23.2 %scatter_custom_fusion.4 = f32[4608,24]{1,0:T(8,128)S(1)} fusion(s32[4096]{0:T(1024)S(1)} %reshape.169, f32[4096,24]{1,0:T(8,128)} %reshape.203, f32[]{:T(128)} %constant.39.clone.1), kind=kCustom, calls=%fused_computation.21 | custom fusion | flops 98304 | bytes 442880 | tf_op jit(solution)/shard_map/scatter-add | solution.py:53
  649.1 4.8 collective-permute-done.15
  654.4 14.9 %gather_fusion.5 = bf16[4096,24]{1,0:T(8,128)(2,1)} fusion(bf16[4608,24]{1,0:T(8,128)(2,1)S(1)} %copy.208, s32[4096]{0:T(1024)S(1)} %broadcast_clamp_fusion), kind=kCustom, calls=%fused_computation.5 | custom fusion | bytes 409600 | tf_op jit(solution)/shard_map/gather | solution.py:68
  680.0 22.4 %scatter_custom_fusion.5 = f32[384,8]{1,0:T(8,128)S(1)} fusion(s32[4096]{0:T(1024)S(1)} %reshape.177, f32[4096,8]{1,0:T(8,128)S(1)} %copy.212, f32[]{:T(128)} %constant.39.clone.1), kind=kCustom, calls=%fused_computation.59 | custom fusion | flops 32768 | bytes 12292 | tf_op jit(solution)/shard_map/scatter-add | solution.py:77
  712.1 6.7 all_gather.19
  719.7 533.7 %all-reduce.10.cloned.1.call-done = f32[64,8,32]{0,2,1:T(8,128)} async-done(((f32[64,8,32]{0,2,1:T(8,128)}), f32[64,8,32]{0,2,1:T(8,128)}) %all-reduce.10.cloned.1.call-update) | async-done | bytes 65552 | tf_op jit(solution)/shard_map/psum | solution.py:112
  (172 shorter events, 142.8 us)
Async XLA Ops:
  7.2 1246.2 %all-reduce.10.cloned.1.call-start = ((), (), s32[]{:S(2)}) async-start(), calls=%async_computation | async-start | bytes 262144 | tf_op jit(solution)/shard_map/psum | solution.py:112
  8.8 8.5 collective-permute-start
  12.6 5.5 collective-permute-start.1
  44.4 27.8 %copy-start = (f32[4096,3]{0,1:T(4,128)S(1)}, f32[4096,3]{0,1:T(4,128)}, u32[]{:S(2)}) copy-start(f32[4096,3]{0,1:T(4,128)} %param.13) | copy-start | bytes 147460
  67.6 8.9 collective-permute-start.2
  77.8 6.3 collective-permute-start.3
  109.2 29.5 %copy-start.6 = (u32[256]{0:T(256)S(1)}, u32[256]{0:T(256)}, u32[]{:S(2)}) copy-start(u32[256]{0:T(256)} %constant.60) | copy-start | bytes 3076
  132.7 7.3 collective-permute-start.4
  137.3 6.2 collective-permute-start.5
  143.7 175.1 %copy-start.4 = (f32[256,8]{0,1:T(8,128)}, f32[256,8]{0,1:T(8,128)S(1)}, u32[]{:S(2)}) copy-start(f32[256,8]{0,1:T(8,128)S(1)} %get-tuple-element.35) | copy-start | bytes 24580
  301.0 2.6 collective-permute-start.6
  302.3 5.5 collective-permute-start.7
  357.4 5.7 collective-permute-start.8
  364.3 6.1 collective-permute-start.9
  419.0 5.4 collective-permute-start.10
  423.0 5.5 collective-permute-start.11
  581.9 5.2 collective-permute-start.12
  585.5 5.5 collective-permute-start.13
  640.6 6.0 collective-permute-start.14
  647.8 6.1 collective-permute-start.15
  679.1 39.7 %copy-start.5 = (s32[256]{0:T(256)S(1)}, s32[256]{0:T(256)}, u32[]{:S(2)}) copy-start(s32[256]{0:T(256)} %param.15) | copy-start | bytes 3076
  702.5 5.4 collective-permute-start.16
  706.5 5.5 collective-permute-start.17
  712.0 542.9 %copy-start.3 = (f32[256,8]{0,1:T(8,128)}, f32[256,8]{0,1:T(8,128)S(1)}, u32[]{:S(2)}) copy-start(f32[256,8]{0,1:T(8,128)S(1)} %compare_select_fusion.2) | copy-start | bytes 24580
  (2 other events, 33.2 us)
Sparse Core Ops, SparseCore 0:
  719.8 533.5 all-reduce.9
